TPU v7x, 32 devices: a whole 2x2x4 slice. The times are simulated.
32 devices in a mesh: row: 16 (over z, y, core), col: 2 (over x).
Axes of the slice: x: 2, y: 2, z: 4, core: 2. Of those that a mesh axis runs over, the one named last changes fastest.
Arguments:
- jacobian: bfloat16 [512, 256, 128], P(('col', 'row')), may hold values from -1.5 to 1.5
- weights: bfloat16 [32, 512, 256], P('row', 'col'), may hold values from 0.25 to 4
- panel_weights: bfloat16 [512, 256], P(('col', 'row')), may hold values from 0.25 to 4
- damping: float32 [32, 128], P('row'), may hold values from 0.01 to 1
- panel_inverse: float32 [128, 128], replicated, may hold values from -0.12 to 0.12
Outputs:
- schur: float32 [4096, 65536], P('row', 'col')
All inputs are finite; a program needn't handle non-finite values.
Results may differ from a plain program's by a relative error of at most 0.0022.
Values may be sent and summed in bfloat16 or wider, within the bound.
No kernel may reach another device: no remote copies, remote signals or barrier semaphores. Data moves between devices by JAX's collectives and lax.ppermute only.
A program may use at most 128 MiB of HBM per device.

v0:
```python
import jax
import jax.numpy as jnp
from jax import lax
from jax.sharding import PartitionSpec as P

HIGHEST = lax.Precision.HIGHEST


def broadcast(value, axis, root):
    mine = lax.axis_index(axis) == root
    return lax.psum(jnp.where(mine, value, jnp.zeros_like(value)), axis)


def shards(jacobian, weights, panel_weights, damping, panel_inverse):
    per_dev, sample_rows, param_width = jacobian.shape
    slab_rows, col_block, _ = weights.shape
    row_count = lax.axis_size("row")
    col_count = lax.axis_size("col")
    row_index = lax.axis_index("row")
    col_index = lax.axis_index("col")
    station_total = col_block * col_count
    panel_id = station_total - 1
    slab_ids = row_index * slab_rows + jnp.arange(slab_rows, dtype=jnp.int32)
    col_base = col_index * col_block
    col_ids = col_base + jnp.arange(col_block, dtype=jnp.int32)
    station_piece = lax.all_gather(jacobian, "row", axis=0, tiled=True)
    how_many = station_piece.shape[0]
    piece_ids = col_base + jnp.arange(how_many, dtype=jnp.int32)
    self_pair = slab_ids[:, None] == piece_ids[None, :]
    scaled = weights.astype(jnp.float32)[..., None] * station_piece.astype(jnp.float32)[None]
    scaled = jnp.where(self_pair[:, :, None, None], 0.0, scaled).astype(jnp.bfloat16)
    gram_part = jnp.einsum(
        "ijra,jrb->iab", scaled, station_piece, preferred_element_type=jnp.float32
    )
    gathered = station_piece
    scaled_all = scaled
    gram_part, gathered, scaled_all = (gram_part, gathered, scaled_all)
    home_col = row_index * slab_rows // col_block
    offset = row_index * slab_rows % col_block
    my_slab = lax.dynamic_slice_in_dim(gathered, offset, slab_rows, 0)
    slab_jac = broadcast(my_slab, "col", home_col)
    coupling = jnp.einsum(
        "ijra,irb->iajb", scaled_all, slab_jac, preferred_element_type=jnp.float32
    )
    gram_sum = lax.psum(gram_part, "col")
    identity = jnp.eye(param_width, dtype=jnp.float32)
    diag_block = (
        gram_sum + identity[None] * (jnp.diagonal(gram_sum, axis1=1, axis2=2) * damping)[:, None, :]
    )
    on_self = slab_ids[:, None] == col_ids[None, :]
    hessian = jnp.where(on_self[:, None, :, None], diag_block[:, :, None, :], coupling)
    local_factor = jnp.einsum(
        "iac,cb->iab",
        hessian[:, :, col_block - 1, :],
        panel_inverse,
        precision=HIGHEST,
        preferred_element_type=jnp.float32,
    )
    panel_factor, panel_jac = (
        broadcast(local_factor.astype(jnp.bfloat16), "col", col_count - 1).astype(
            local_factor.dtype
        ),
        broadcast(gathered[col_block - 1], "col", col_count - 1),
    )
    own_ids = (col_index * row_count + row_index) * per_dev + jnp.arange(per_dev, dtype=jnp.int32)
    scaled_rows = panel_weights.astype(jnp.float32)[..., None] * jacobian.astype(jnp.float32)
    scaled_rows = jnp.where((own_ids == panel_id)[:, None, None], 0.0, scaled_rows).astype(
        jnp.bfloat16
    )
    row_part = jnp.einsum("jra,rb->jab", scaled_rows, panel_jac, preferred_element_type=jnp.float32)
    station_piece = lax.all_gather(row_part.astype(jnp.bfloat16), "row", axis=0, tiled=True).astype(
        jnp.float32
    )
    how_many = station_piece.shape[0]
    current = lax.slice_in_dim(hessian, 0, how_many, axis=2)
    correction = jnp.einsum(
        "iac,jcb->iajb",
        panel_factor,
        station_piece,
        precision=HIGHEST,
        preferred_element_type=jnp.float32,
    )
    piece_ids = col_base + jnp.arange(how_many, dtype=jnp.int32)
    result = jnp.where(
        (piece_ids == panel_id)[None, None, :, None],
        panel_factor[:, :, None, :],
        current - correction,
    )
    return result.reshape(slab_rows * param_width, how_many * param_width)


def solution(mesh):
    return jax.shard_map(
        shards,
        mesh=mesh,
        in_specs=(
            P(("col", "row"), None, None),
            P("row", "col", None),
            P(("col", "row"), None),
            P("row", None),
            P(),
        ),
        out_specs=P("row", "col"),
        check_vma=False,
    )
```

profile of v0, /device:TPU:0, one launch (start us, length us, event | category | flops | bytes accessed | tf_op | source)
XLA Modules:
  0.0 486.4 jit_solution(10741653485367392175)
XLA Ops:
  6.5 0.0 copy-start
  6.5 0.0 all-gather.3.cloned.1.call-start
  6.5 0.7 all-gather.3.cloned.1.call-update
  7.3 0.0 all-reduce.5.cloned.1.call-start
  7.3 1.0 convert_element_type.35
  8.4 0.1 broadcast_compare_fusion
  8.5 130.7 %all-gather.3.cloned.1.call-done = bf16[256,256,128]{2,1,0:T(8,128)(2,1)} async-done(((bf16[16,256,128]{2,1,0:T(8,128)(2,1)}), bf16[256,256,128]{2,1,0:T(8,128)(2,1)}) %all-gather.3.cloned.1.call-update) | async-done | bytes 16777232 | tf_op jit(solution)/shard_map/all_gather | solution.py:26
  139.1 0.9 constant_dynamic-slice_fusion
  140.1 0.1 copy.53
  140.2 9.4 %convert_element_type.36 = f32[256,256,128]{2,1,0:T(8,128)S(1)} convert(bf16[256,256,128]{2,1,0:T(8,128)(2,1)} %all-gather.3.cloned.1.call-done) | non-fusion elementwise | flops 8388608 | bytes 50331648 | tf_op jit(solution)/shard_map/convert_element_type | solution.py:30
  149.6 0.0 copy-start.1
  149.6 11.7 %copy-done.1 = f32[256,256,128]{2,1,0:T(8,128)} copy-done((f32[256,256,128]{2,1,0:T(8,128)}, f32[256,256,128]{2,1,0:T(8,128)S(1)}, u32[]{:S(2)}) %copy-start.1) | copy-done | bytes 33554456
  161.3 0.0 copy-start.5
  161.3 47.9 %fusion.12 = f32[2,128,128]{2,1,0:T(8,128)} fusion(bf16[256,256,128]{2,1,0:T(8,128)(2,1)} %all-gather.3.cloned.1.call-done, f32[256,256,128]{2,1,0:T(8,128)S(1)} %convert_element_type.36, f32[2,256,256]{2,1,0:T(8,128)S(1)} %convert_element_type.35, pred[2,256]{1,0:T(4,128)(4,1)S(1)} %broadcast_compare_fusion), kind=kOutput, calls=%fused_computation.19 | convolution fusion | flops 4345298944 | bytes 50987520 | tf_op jit(solution)/shard_map/ijra,jrb->iab/dot_general | solution.py:32
  209.2 0.0 all-reduce.5.cloned.1.call-update
  209.2 0.0 all-reduce.7.cloned.1.call-start
  209.2 0.7 broadcast_select_fusion
  209.9 0.0 all-reduce.7.cloned.1.call-update
  209.9 0.0 all-reduce.9.cloned.1.call-start
  210.0 1.5 fusion.20
  211.5 17.5 %all-reduce.5.cloned.1.call-done = f32[2,128,128]{2,1,0:T(8,128)} async-done(((f32[2,128,128]{2,1,0:T(8,128)}), f32[2,128,128]{2,1,0:T(8,128)}) %all-reduce.5.cloned.1.call-update) | async-done | bytes 131088 | tf_op jit(solution)/shard_map/psum | solution.py:45
  228.9 5.5 %copy.37 = f32[2,128,128]{0,2,1:T(8,128)} copy(f32[2,128,128]{2,1,0:T(8,128)} %all-reduce.5.cloned.1.call-done) | data formatting | bytes 262144 | tf_op jit(solution)/shard_map/psum | solution.py:45
  234.4 1.8 gather_fusion
  236.2 0.1 copy.38
  236.3 0.0 copy-done.5
  236.3 0.9 multiply_add_fusion
  237.2 0.1 copy.39
  237.3 0.0 copy-start.4
  237.3 0.0 copy-start.3
  237.4 15.3 %all-reduce.7.cloned.1.call-done = bf16[2,256,128]{1,2,0:T(8,128)(2,1)} async-done(((bf16[2,256,128]{1,2,0:T(8,128)(2,1)}), bf16[2,256,128]{1,2,0:T(8,128)(2,1)}) %all-reduce.7.cloned.1.call-update) | async-done | bytes 131088 | tf_op jit(solution)/shard_map/psum | solution.py:11
  252.7 23.6 %bitcast_select_fusion = f32[2,128,256,128]{1,3,2,0:T(8,128)S(1)} fusion(f32[2,128,128]{1,2,0:T(8,128)S(1)} %copy.39, pred[2,256]{1,0:T(4,128)(4,1)S(1)} %broadcast_compare_fusion, f32[256,256,128]{2,1,0:T(8,128)} %copy-done.1, f32[2,256,256]{2,1,0:T(8,128)S(1)} %convert_element_type.35, bf16[2,256,128]{1,2,0:T(8,128)(2,1)} %all-reduce.7.cloned.1.call-done), kind=kOutput, calls=%fused_computation.5 | convolution fusion | flops 4353687552 | bytes 67895808 | tf_op jit(solution)/shard_map/ijra,irb->iajb/dot_general | solution.py:42
  276.3 0.0 copy-start.2
  276.3 11.7 %copy-done.2 = f32[2,128,256,128]{1,3,2,0:T(8,128)} copy-done((f32[2,128,256,128]{1,3,2,0:T(8,128)}, f32[2,128,256,128]{1,3,2,0:T(8,128)S(1)}, u32[]{:S(2)}) %copy-start.2) | copy-done | bytes 33554456
  288.0 0.0 copy-done
  288.0 1.0 fusion.15
  289.0 0.0 all-reduce.9.cloned.1.call-update
  289.1 0.2 all-gather.5.cloned.1.call-start
  289.3 0.0 copy-done.4
  289.3 21.5 %all-reduce.9.cloned.1.call-done = (bf16[2,128,128]{2,1,0:T(8,128)(2,1)}, bf16[256,128]{1,0:T(8,128)(2,1)}) async-done(((bf16[2,128,128]{2,1,0:T(8,128)(2,1)}, bf16[256,128]{1,0:T(8,128)(2,1)}), (bf16[2,128,128]{2,1,0:T(8,128)(2,1)}, bf16[256,128]{1,0:T(8,128)(2,1)})) %all-reduce.9.cloned.1.call-update) | async-done | bytes 131088 | tf_op jit(solution)/shard_map/psum | solution.py:11
  310.8 0.0 copy-done.3
  310.8 2.9 convolution_convert_fusion
  313.7 0.0 all-gather.5.cloned.1.call-update
  313.7 0.9 copy.42
  314.7 74.1 %all-gather.5.cloned.1.call-done = bf16[256,128,128]{2,1,0:T(8,128)(2,1)} async-done(((bf16[16,128,128]{2,1,0:T(8,128)(2,1)}), bf16[256,128,128]{2,1,0:T(8,128)(2,1)}) %all-gather.5.cloned.1.call-update) | async-done | bytes 8388624 | tf_op jit(solution)/shard_map/all_gather | solution.py:71
  388.8 28.2 %subtract_select_fusion = f32[2,128,256,128]{1,3,2,0:T(8,128)} fusion(f32[2,128,256,128]{1,3,2,0:T(8,128)} %copy-done.2, f32[2,128,128]{1,2,0:T(8,128)S(1)} %copy.42, pred[256]{0:T(512)(128)(4,1)S(1)} %broadcast_compare_fusion.1, bf16[256,128,128]{2,1,0:T(8,128)(2,1)} %all-gather.5.cloned.1.call-done, bf16[2,128,128]{2,1,0:T(8,128)(2,1)} %get-tuple-element.5), kind=kOutput, calls=%fused_computation.6 | convolution fusion | flops 2164260864 | bytes 75694336 | tf_op jit(solution)/shard_map/iac,jcb->iajb/dot_general | solution.py:76
  417.0 31.1 %copy.45 = f32[2,128,256,128]{3,2,1,0:T(8,128)} copy(f32[2,128,256,128]{1,3,2,0:T(8,128)} %subtract_select_fusion) | data formatting | bytes 67108864 | tf_op jit(solution)/shard_map/jit(_where)/select_n | solution.py:84
  448.1 31.8 %copy.56 = f32[32,8,256,128]{3,1,2,0:T(8,128)} copy(f32[32,8,256,128]{3,2,1,0:T(8,128)} %bitcast.47) | data formatting | bytes 67108864
  (8 shorter events, 0.1 us)
Async XLA Ops:
  6.5 281.5 %copy-start = (f32[128,128]{1,0:T(8,128)S(1)}, f32[128,128]{1,0:T(8,128)}, u32[]{:S(2)}) copy-start(f32[128,128]{1,0:T(8,128)} %param.9) | copy-start | bytes 196612
  6.5 132.6 %all-gather.3.cloned.1.call-start = ((), (), s32[]{:S(2)}) async-start(), calls=%async_computation | async-start | bytes 17825792 | tf_op jit(solution)/shard_map/all_gather | solution.py:26
  7.3 221.7 %all-reduce.5.cloned.1.call-start = ((), (), s32[]{:S(2)}) async-start(), calls=%async_computation.1 | async-start | bytes 262144 | tf_op jit(solution)/shard_map/psum | solution.py:45
  149.6 11.7 %copy-start.1 = (f32[256,256,128]{2,1,0:T(8,128)}, f32[256,256,128]{2,1,0:T(8,128)S(1)}, u32[]{:S(2)}) copy-start(f32[256,256,128]{2,1,0:T(8,128)S(1)} %convert_element_type.36) | copy-start | bytes 100663296
  161.3 75.0 %copy-start.5 = (f32[2,128]{1,0:T(2,128)S(1)}, f32[2,128]{1,0:T(2,128)}, u32[]{:S(2)}) copy-start(f32[2,128]{1,0:T(2,128)} %param.8) | copy-start | bytes 3076
  209.2 43.5 %all-reduce.7.cloned.1.call-start = ((), (), s32[]{:S(2)}) async-start(), calls=%async_computation.2 | async-start | bytes 262144 | tf_op jit(solution)/shard_map/psum | solution.py:11
  209.9 100.9 %all-reduce.9.cloned.1.call-start = ((), (), s32[]{:S(2)}) async-start(), calls=%async_computation.4 | async-start | bytes 262144 | tf_op jit(solution)/shard_map/psum | solution.py:11
  237.3 52.0 %copy-start.4 = (bf16[16,256]{1,0:T(8,128)(2,1)S(1)}, bf16[16,256]{1,0:T(8,128)(2,1)}, u32[]{:S(2)}) copy-start(bf16[16,256]{1,0:T(8,128)(2,1)} %param.7) | copy-start | bytes 24580
  237.3 73.5 %copy-start.3 = (bf16[16,256,128]{2,1,0:T(8,128)(2,1)S(1)}, bf16[16,256,128]{2,1,0:T(8,128)(2,1)}, u32[]{:S(2)}) copy-start(bf16[16,256,128]{2,1,0:T(8,128)(2,1)} %param.5) | copy-start | bytes 3145732
  276.3 11.7 %copy-start.2 = (f32[2,128,256,128]{1,3,2,0:T(8,128)}, f32[2,128,256,128]{1,3,2,0:T(8,128)S(1)}, u32[]{:S(2)}) copy-start(f32[2,128,256,128]{1,3,2,0:T(8,128)S(1)} %bitcast_select_fusion) | copy-start | bytes 100663296
  289.1 99.7 %all-gather.5.cloned.1.call-start = ((), (), s32[]{:S(2)}) async-start(), calls=%async_computation.3 | async-start | bytes 8912896 | tf_op jit(solution)/shard_map/all_gather | solution.py:71
Sparse Core Ops, SparseCore 0:
  9.5 129.5 all-gather.2
  209.3 19.5 all-reduce.4
  231.2 21.4 all-reduce.6
  289.2 21.5 all-reduce.8
  313.8 74.8 all-gather.4
where the time goes:
time: 488 us; the launch traced here: 486 us
  waiting for transfers between devices  260 us (53%)
  matrix products  104 us (21%)
  local copies, waits for them, and re-layouts  95.7 us (20%)
  other arithmetic  13.6 us (3%)
  between operations  13.3 us (3%)
    all_gather x1, waiting for transfers between devices, shards(): station_piece = lax.all_gather(jacobian, 'row', axis=0, tiled=True)  131 us
    all_gather x1, waiting for transfers between devices, shards(): lax.all_gather(row_part.astype(jnp.bfloat16), 'row', axis=0, tiled=True)  74.1 us
    unnamed x14, local copies, waits for them, and re-layouts  55.3 us
    dot_general x1, matrix products, shards(): jnp.einsum('ijra,jrb->iab', scaled, station_piece, preferred_element_type...  47.9 us
    psum x2, waiting for transfers between devices, broadcast(): return lax.psum(jnp.where(mine, value, jnp.zeros_like(value)), axis)  36.8 us
    select_n x1, local copies, waits for them, and re-layouts, shards(): jnp.where((piece_ids == panel_id)[None, None, :, None], panel_factor[:, :...  31.1 us
    dot_general x1, matrix products, shards(): jnp.einsum('iac,jcb->iajb', panel_factor, station_piece, precision=HIGHES...  28.2 us
    dot_general x1, matrix products, shards(): jnp.einsum('ijra,irb->iajb', scaled_all, slab_jac, preferred_element_type...  23.6 us
  transfers between devices with their start and end apart: 5, of which 5 were waited for; matrix products, arithmetic and copies ran while one was open for 3% of the time, Pallas kernels for 0%

commit v1 on v0

--- a/solution.py
+++ b/solution.py
@@ -2,8 +2,27 @@
 import jax.numpy as jnp
 from jax import lax
 from jax.sharding import PartitionSpec as P
+from jax.lax import axis_index, axis_size, ppermute
 
 HIGHEST = lax.Precision.HIGHEST
+
+
+def produce_groups_over_axis(t0, on_dim):
+    y1 = list(t0.shape[1:])
+    y1[on_dim] *= t0.shape[0]
+    return jnp.moveaxis(t0, 0, on_dim).reshape(y1)
+
+
+def _watch_forms(xx, comm_axis):
+    many = axis_size(comm_axis)
+    upper = xx[None]
+    for w in range(many.bit_length() - 1):
+        piece_now = 1 << w
+        h_now = ppermute(upper, comm_axis, perm=[(c, c ^ piece_now) for c in range(many)])
+        fresh = jnp.stack([upper, h_now])
+        front = axis_index(comm_axis) >> w & 1
+        upper = jnp.where(front == 0, fresh, fresh[::-1]).reshape(-1, *xx.shape)
+    return upper
 
 
 def broadcast(value, axis, root):
@@ -68,9 +87,11 @@
         jnp.bfloat16
     )
     row_part = jnp.einsum("jra,rb->jab", scaled_rows, panel_jac, preferred_element_type=jnp.float32)
-    station_piece = lax.all_gather(row_part.astype(jnp.bfloat16), "row", axis=0, tiled=True).astype(
-        jnp.float32
-    )
+
+    def work_tables_up(vec, arr, at_axis):
+        return produce_groups_over_axis(_watch_forms(vec, arr), at_axis)
+
+    station_piece = work_tables_up(row_part.astype(jnp.bfloat16), "row", 0).astype(jnp.float32)
     how_many = station_piece.shape[0]
     current = lax.slice_in_dim(hessian, 0, how_many, axis=2)
     correction = jnp.einsum(

time: 488 us -> 697 us (1.43)
  waiting for transfers between devices: 260 us -> 437 us
  other arithmetic: 13.6 us -> 41.6 us
    ppermute x0 -> x4, waiting for transfers between devices: none -> 251 us  [_watch_forms(): ppermute(upper, comm_axis, perm=[(c, c ^ piece_now) for c in range(many)])]
    all_gather x1 -> x0, waiting for transfers between devices: 74.1 us -> none  [shards(): lax.all_gather(row_part.astype(jnp.bfloat16), 'row', axis=0, tiled=True)]
    select_n x0 -> x3, other arithmetic: none -> 18.6 us  [_watch_forms(): upper = jnp.where(front == 0, fresh, fresh[::-1]).reshape(-1, *xx.shape)]
    another operation x0 -> x5, other arithmetic: none -> 10.4 us  [_watch_forms(): fresh = jnp.stack([upper, h_now])]
    unnamed x14 -> x20, local copies, waits for them, and re-layouts: 55.3 us -> 55.4 us
  transfers between devices with their start and end apart: 5 -> 8, of which waited for: 5 -> 8; matrix products, arithmetic and copies ran while one was open for 3% -> 2% of each run, Pallas kernels for 0% -> 0%
where the time goes in v1:
time: 697 us; the launch traced here: 696 us
  waiting for transfers between devices  437 us (63%)
  matrix products  103 us (15%)
  local copies, waits for them, and re-layouts  95.1 us (14%)
  other arithmetic  41.6 us (6%)
  between operations  13.4 us (2%)
    ppermute x4, waiting for transfers between devices, _watch_forms(): ppermute(upper, comm_axis, perm=[(c, c ^ piece_now) for c in range(many)])  251 us
    all_gather x1, waiting for transfers between devices, shards(): station_piece = lax.all_gather(jacobian, 'row', axis=0, tiled=True)  131 us
    unnamed x20, local copies, waits for them, and re-layouts  55.4 us
    dot_general x1, matrix products, shards(): jnp.einsum('ijra,jrb->iab', scaled, station_piece, preferred_element_type...  47.9 us
    psum x2, waiting for transfers between devices, broadcast(): return lax.psum(jnp.where(mine, value, jnp.zeros_like(value)), axis)  37.8 us
    select_n x1, local copies, waits for them, and re-layouts, shards(): jnp.where((piece_ids == panel_id)[None, None, :, None], panel_factor[:, :...  31.2 us
    dot_general x1, matrix products, shards(): jnp.einsum('iac,jcb->iajb', panel_factor, station_piece, precision=HIGHES...  28.2 us
    dot_general x1, matrix products, shards(): jnp.einsum('ijra,irb->iajb', scaled_all, slab_jac, preferred_element_type...  23.6 us
  transfers between devices with their start and end apart: 8, of which 8 were waited for; matrix products, arithmetic and copies ran while one was open for 2% of the time, Pallas kernels for 0%

profile of v1, /device:TPU:0, one launch (start us, length us, event | category | flops | bytes accessed | tf_op | source)
XLA Modules:
  0.0 695.9 jit_solution(18171121005672023169)
XLA Ops:
  6.5 0.7 all-gather.2.cloned.1.call-update
  7.3 0.0 all-reduce.5.cloned.1.call-start
  7.3 1.0 convert_element_type.35
  8.4 0.1 broadcast_compare_fusion
  8.5 130.7 %all-gather.2.cloned.1.call-done = bf16[256,256,128]{2,1,0:T(8,128)(2,1)} async-done(((bf16[16,256,128]{2,1,0:T(8,128)(2,1)}), bf16[256,256,128]{2,1,0:T(8,128)(2,1)}) %all-gather.2.cloned.1.call-update) | async-done | bytes 16777232 | tf_op jit(solution)/shard_map/all_gather | solution.py:45
  139.1 0.9 constant_dynamic-slice_fusion
  140.1 0.1 copy.55
  140.2 9.4 %convert_element_type.36 = f32[256,256,128]{2,1,0:T(8,128)S(1)} convert(bf16[256,256,128]{2,1,0:T(8,128)(2,1)} %all-gather.2.cloned.1.call-done) | non-fusion elementwise | flops 8388608 | bytes 50331648 | tf_op jit(solution)/shard_map/convert_element_type | solution.py:49
  149.6 11.7 %copy-done.2 = f32[256,256,128]{2,1,0:T(8,128)} copy-done((f32[256,256,128]{2,1,0:T(8,128)}, f32[256,256,128]{2,1,0:T(8,128)S(1)}, u32[]{:S(2)}) %copy-start.2) | copy-done | bytes 33554456
  161.3 47.9 %fusion.11 = f32[2,128,128]{2,1,0:T(8,128)} fusion(bf16[256,256,128]{2,1,0:T(8,128)(2,1)} %all-gather.2.cloned.1.call-done, f32[256,256,128]{2,1,0:T(8,128)S(1)} %convert_element_type.36, f32[2,256,256]{2,1,0:T(8,128)S(1)} %convert_element_type.35, pred[2,256]{1,0:T(4,128)(4,1)S(1)} %broadcast_compare_fusion), kind=kOutput, calls=%fused_computation.25 | convolution fusion | flops 4345298944 | bytes 50987520 | tf_op jit(solution)/shard_map/ijra,jrb->iab/dot_general | solution.py:51
  209.2 0.0 all-reduce.5.cloned.1.call-update
  209.2 0.0 all-reduce.7.cloned.1.call-start
  209.2 0.7 broadcast_select_fusion
  209.9 0.0 all-reduce.7.cloned.1.call-update
  209.9 0.0 all-reduce.9.cloned.1.call-start
  210.0 1.5 fusion.21
  211.4 17.5 %all-reduce.5.cloned.1.call-done = f32[2,128,128]{2,1,0:T(8,128)} async-done(((f32[2,128,128]{2,1,0:T(8,128)}), f32[2,128,128]{2,1,0:T(8,128)}) %all-reduce.5.cloned.1.call-update) | async-done | bytes 131088 | tf_op jit(solution)/shard_map/psum | solution.py:64
  228.9 5.6 copy.39
  234.5 1.8 gather_fusion
  236.3 0.1 copy.40
  236.4 0.1 copy.41
  236.5 16.1 %all-reduce.7.cloned.1.call-done = bf16[2,256,128]{1,2,0:T(8,128)(2,1)} async-done(((bf16[2,256,128]{1,2,0:T(8,128)(2,1)}), bf16[2,256,128]{1,2,0:T(8,128)(2,1)}) %all-reduce.7.cloned.1.call-update) | async-done | bytes 131088 | tf_op jit(solution)/shard_map/psum | solution.py:30
  252.7 23.6 %bitcast_select_fusion = f32[2,128,256,128]{1,3,2,0:T(8,128)S(1)} fusion(f32[2,128,128]{1,2,0:T(8,128)S(1)} %copy.41, pred[2,256]{1,0:T(4,128)(4,1)S(1)} %broadcast_compare_fusion, f32[256,256,128]{2,1,0:T(8,128)} %copy-done.2, f32[2,256,256]{2,1,0:T(8,128)S(1)} %convert_element_type.35, bf16[2,256,128]{1,2,0:T(8,128)(2,1)} %all-reduce.7.cloned.1.call-done), kind=kOutput, calls=%fused_computation.5 | convolution fusion | flops 4353687552 | bytes 67895808 | tf_op jit(solution)/shard_map/ijra,irb->iajb/dot_general | solution.py:61
  276.3 11.7 %copy-done.3 = f32[2,128,256,128]{1,3,2,0:T(8,128)} copy-done((f32[2,128,256,128]{1,3,2,0:T(8,128)}, f32[2,128,256,128]{1,3,2,0:T(8,128)S(1)}, u32[]{:S(2)}) %copy-start.3) | copy-done | bytes 33554456
  288.0 1.0 fusion.14
  289.0 0.0 all-reduce.9.cloned.1.call-update
  289.1 21.7 %all-reduce.9.cloned.1.call-done = (bf16[2,128,128]{2,1,0:T(8,128)(2,1)}, bf16[256,128]{1,0:T(8,128)(2,1)}) async-done(((bf16[2,128,128]{2,1,0:T(8,128)(2,1)}, bf16[256,128]{1,0:T(8,128)(2,1)}), (bf16[2,128,128]{2,1,0:T(8,128)(2,1)}, bf16[256,128]{1,0:T(8,128)(2,1)})) %all-reduce.9.cloned.1.call-update) | async-done | bytes 131088 | tf_op jit(solution)/shard_map/psum | solution.py:30
  310.8 2.2 convolution_convert_fusion
  312.9 0.1 collective-permute-start
  313.0 1.9 collective-permute-done
  314.9 0.1 pad_maximum_fusion.3
  315.0 0.6 fusion.19
  315.6 1.5 collective-permute-start.1
  317.2 23.7 %collective-permute-done.1 = bf16[2,16,128,128]{3,2,1,0:T(8,128)(2,1)S(1)} collective-permute-done((bf16[2,16,128,128]{3,2,1,0:T(8,128)(2,1)S(1)}, bf16[2,16,128,128]{3,2,1,0:T(8,128)(2,1)S(1)}, u32[]{:S(2)}, u32[]{:S(2)}) %collective-permute-start.1) | collective-permute-done | bytes 1048608 | tf_op jit(solution)/shard_map/ppermute | solution.py:21
  340.9 0.2 pad_maximum_fusion.2
  341.1 0.6 reverse_select_fusion.2
  341.7 1.5 collective-permute-start.2
  343.2 45.5 %collective-permute-done.2 = bf16[4,16,128,128]{3,2,1,0:T(8,128)(2,1)} collective-permute-done((bf16[4,16,128,128]{3,2,1,0:T(8,128)(2,1)S(1)}, bf16[4,16,128,128]{3,2,1,0:T(8,128)(2,1)}, u32[]{:S(2)}, u32[]{:S(2)}) %collective-permute-start.2) | collective-permute-done | bytes 2097184 | tf_op jit(solution)/shard_map/ppermute | solution.py:21
  388.7 2.0 pad_maximum_fusion.1
  390.7 3.1 reverse_select_fusion.1
  393.8 2.4 collective-permute-start.3
  396.2 0.1 copy.44
  396.3 179.4 %collective-permute-done.3 = bf16[8,16,128,128]{3,2,1,0:T(8,128)(2,1)} collective-permute-done((bf16[8,16,128,128]{3,2,1,0:T(8,128)(2,1)}, bf16[8,16,128,128]{3,2,1,0:T(8,128)(2,1)}, u32[]{:S(2)}, u32[]{:S(2)}) %collective-permute-start.3) | collective-permute-done | bytes 4194336 | tf_op jit(solution)/shard_map/ppermute | solution.py:21
  575.8 7.5 %pad_maximum_fusion = bf16[2,8,16,128,128]{4,3,2,1,0:T(8,128)(2,1)} fusion(bf16[1,8,16,128,128]{4,3,2,1,0:T(8,128)(2,1)} %bitcast.25, bf16[1,8,16,128,128]{4,3,2,1,0:T(8,128)(2,1)} %bitcast.23), kind=kLoop, calls=%fused_computation.17 | loop fusion | flops 4194304 | bytes 16777216 | tf_op jit(solution)/shard_map/stack | solution.py:22
  583.2 14.9 %reverse_select_fusion = bf16[2,8,16,128,128]{4,3,2,1,0:T(8,128)(2,1)} fusion(bf16[2,8,16,128,128]{4,3,2,1,0:T(8,128)(2,1)} %pad_maximum_fusion, pred[]{:T(512)S(6)} %eq.81), kind=kLoop, calls=%fused_computation.16 | loop fusion | flops 4194304 | bytes 16777216 | tf_op jit(solution)/shard_map/jit(_where)/select_n | solution.py:24
  598.2 28.2 %subtract_select_fusion = f32[2,128,256,128]{1,3,2,0:T(8,128)} fusion(f32[2,128,256,128]{1,3,2,0:T(8,128)} %copy-done.3, bf16[256,128,128,1]{2,1,0,3:T(8,128)(2,1)} %bitcast.63, f32[2,128,128]{1,2,0:T(8,128)S(1)} %copy.44, pred[256]{0:T(512)(128)(4,1)S(1)} %broadcast_compare_fusion.1, bf16[2,128,128]{2,1,0:T(8,128)(2,1)S(1)} %copy-done.6), kind=kOutput, calls=%fused_computation.6 | convolution fusion | flops 2164260864 | bytes 75694336 | tf_op jit(solution)/shard_map/iac,jcb->iajb/dot_general | solution.py:97
  626.3 31.2 %copy.47 = f32[2,128,256,128]{3,2,1,0:T(8,128)} copy(f32[2,128,256,128]{1,3,2,0:T(8,128)} %subtract_select_fusion) | data formatting | bytes 67108864 | tf_op jit(solution)/shard_map/jit(_where)/select_n | solution.py:105
  657.5 31.8 %copy.58 = f32[32,8,256,128]{3,1,2,0:T(8,128)} copy(f32[32,8,256,128]{3,2,1,0:T(8,128)} %bitcast.62) | data formatting | bytes 67108864
  (26 shorter events, 0.1 us)
Async XLA Ops:
  6.5 281.5 %copy-start = (f32[128,128]{1,0:T(8,128)S(1)}, f32[128,128]{1,0:T(8,128)}, u32[]{:S(2)}) copy-start(f32[128,128]{1,0:T(8,128)} %param.9) | copy-start | bytes 196612
  6.5 132.6 %all-gather.2.cloned.1.call-start = ((), (), s32[]{:S(2)}) async-start(), calls=%async_computation | async-start | bytes 17825792 | tf_op jit(solution)/shard_map/all_gather | solution.py:45
  7.3 221.7 %all-reduce.5.cloned.1.call-start = ((), (), s32[]{:S(2)}) async-start(), calls=%async_computation.1 | async-start | bytes 262144 | tf_op jit(solution)/shard_map/psum | solution.py:64
  149.6 11.7 %copy-start.2 = (f32[256,256,128]{2,1,0:T(8,128)}, f32[256,256,128]{2,1,0:T(8,128)S(1)}, u32[]{:S(2)}) copy-start(f32[256,256,128]{2,1,0:T(8,128)S(1)} %convert_element_type.36) | copy-start | bytes 100663296
  209.1 27.2 %copy-start.8 = (f32[2,128]{1,0:T(2,128)S(1)}, f32[2,128]{1,0:T(2,128)}, u32[]{:S(2)}) copy-start(f32[2,128]{1,0:T(2,128)} %param.8) | copy-start | bytes 3076
  209.2 43.5 %all-reduce.7.cloned.1.call-start = ((), (), s32[]{:S(2)}) async-start(), calls=%async_computation.2 | async-start | bytes 262144 | tf_op jit(solution)/shard_map/psum | solution.py:30
  209.9 100.8 %all-reduce.9.cloned.1.call-start = ((), (), s32[]{:S(2)}) async-start(), calls=%async_computation.3 | async-start | bytes 262144 | tf_op jit(solution)/shard_map/psum | solution.py:30
  228.9 7.5 %copy-start.5 = (f32[2,128,128]{2,1,0:T(8,128)S(1)}, f32[2,128,128]{2,1,0:T(8,128)}, u32[]{:S(2)}) copy-start(f32[2,128,128]{2,1,0:T(8,128)} %all-reduce.5.cloned.1.call-done) | copy-start | bytes 393220
  236.5 52.5 %copy-start.7 = (bf16[16,256]{1,0:T(8,128)(2,1)S(1)}, bf16[16,256]{1,0:T(8,128)(2,1)}, u32[]{:S(2)}) copy-start(bf16[16,256]{1,0:T(8,128)(2,1)} %param.7) | copy-start | bytes 24580
  236.5 74.2 %copy-start.4 = (bf16[16,256,128]{2,1,0:T(8,128)(2,1)S(1)}, bf16[16,256,128]{2,1,0:T(8,128)(2,1)}, u32[]{:S(2)}) copy-start(bf16[16,256,128]{2,1,0:T(8,128)(2,1)} %param.5) | copy-start | bytes 3145732
  276.3 11.7 %copy-start.3 = (f32[2,128,256,128]{1,3,2,0:T(8,128)}, f32[2,128,256,128]{1,3,2,0:T(8,128)S(1)}, u32[]{:S(2)}) copy-start(f32[2,128,256,128]{1,3,2,0:T(8,128)S(1)} %bitcast_select_fusion) | copy-start | bytes 100663296
  312.9 2.0 collective-permute-start
  315.6 25.3 %collective-permute-start.1 = (bf16[2,16,128,128]{3,2,1,0:T(8,128)(2,1)S(1)}, bf16[2,16,128,128]{3,2,1,0:T(8,128)(2,1)S(1)}, u32[]{:S(2)}, u32[]{:S(2)}) collective-permute-start(bf16[2,16,128,128]{3,2,1,0:T(8,128)(2,1)S(1)} %get-tuple-element.8), channel_id=1, source_target_pairs={{0,4},{2,6},{4,0},{6,2},{8,12},{10,14},{12,8},{14,10},{16,20},{18,... | collective-permute-start | bytes 3145736 | tf_op jit(solution)/shard_map/ppermute | solution.py:21
  341.7 47.0 %collective-permute-start.2 = (bf16[4,16,128,128]{3,2,1,0:T(8,128)(2,1)S(1)}, bf16[4,16,128,128]{3,2,1,0:T(8,128)(2,1)}, u32[]{:S(2)}, u32[]{:S(2)}) collective-permute-start(bf16[4,16,128,128]{3,2,1,0:T(8,128)(2,1)S(1)} %bitcast.64), channel_id=1, source_target_pairs={{0,8},{2,10},{4,12},{6,14},{8,0},{10,2},{12,4},{14,6},{16,24},{18,... | collective-permute-start | bytes 6291464 | tf_op jit(solution)/shard_map/ppermute | solution.py:21
  388.7 7.5 %copy-start.6 = (bf16[2,128,128]{2,1,0:T(8,128)(2,1)S(1)}, bf16[2,128,128]{2,1,0:T(8,128)(2,1)}, u32[]{:S(2)}) copy-start(bf16[2,128,128]{2,1,0:T(8,128)(2,1)} %get-tuple-element.5) | copy-start | bytes 196612
  393.8 182.0 %collective-permute-start.3 = (bf16[8,16,128,128]{3,2,1,0:T(8,128)(2,1)}, bf16[8,16,128,128]{3,2,1,0:T(8,128)(2,1)}, u32[]{:S(2)}, u32[]{:S(2)}) collective-permute-start(bf16[8,16,128,128]{3,2,1,0:T(8,128)(2,1)} %bitcast.24), channel_id=1, source_target_pairs={{0,16},{2,18},{4,20},{6,22},{8,24},{10,26},{12,28},{14,30},{16,0},... | collective-permute-start | bytes 12582920 | tf_op jit(solution)/shard_map/ppermute | solution.py:21
  657.5 31.8 %copy-start.1 = (f32[128,128]{1,0:T(8,128)S(1)}, f32[128,128]{1,0:T(8,128)}, u32[]{:S(2)}) copy-start(f32[128,128]{1,0:T(8,128)} %param.9) | copy-start | bytes 196612
Sparse Core Ops, SparseCore 0:
  9.5 129.5 all-gather.1
  209.3 19.5 all-reduce.4
  231.2 21.4 all-reduce.6
  289.1 21.5 all-reduce.8
